TPU v7x, 128 devices: a whole 4x4x4 slice. The times are simulated.
128 devices in a mesh: rel: 4 (over z), ent: 32 (over y, x, core).
Axes of the slice: x: 4, y: 4, z: 4, core: 2. Of those that a mesh axis runs over, the one named last changes fastest.
Arguments:
- features: bfloat16 [16384, 512], P('ent'), may hold values from -6 to 6
- w_self: bfloat16 [512, 512], replicated, may hold values from -0.25 to 0.25
- basis_mats: bfloat16 [16384, 512], replicated, may hold values from -0.046875 to 0.046875
- basis_coeffs: float32 [1000, 32], replicated, may hold values from -5 to 5
- group_rels: int32 [1000], P('rel'), may hold values from 0 to 999, each once
- rel_local: int32 [65536], P(('rel', 'ent')), may hold values from 0 to 249
- edge_src: int32 [65536], P(('rel', 'ent')), may hold values from 0 to 16383, as said below
- edge_dst: int32 [65536], P(('rel', 'ent')), may hold values from 0 to 16383, as said below
- block_counts: int32 [4, 32, 32], P('rel', 'ent'), may hold values from 1 to 16, as said below
- cotangent: bfloat16 [16384, 512], P('ent'), may hold values from -6 to 6
Outputs:
- activations: bfloat16 [16384, 512], P('ent')
- grad_features: bfloat16 [16384, 512], P('ent')
- grad_basis: float32 [16384, 512], P(('rel', 'ent'))
Inputs may be any that keep to these rules, and one draw needn't show every extreme that they name: `edge_src`: slot i's source is owned by ent index (i // 512) % 32: it lies in [that index * 512, that index * 512 + 512). `edge_dst`: slot i's destination is owned by block index k = (i % 512) // 16: it lies in [k * 512, k * 512 + 512); within each aligned block of 16 slots the destinations are non-decreasing; the live slots of a block are its first block_counts ones. `block_counts`: one relation group, drawn from the seed, has every block full.
All inputs are finite; a program needn't handle non-finite values.
Results may differ from a plain program's by a relative error of at most 0.0059.
Values may be sent and summed in bfloat16 or wider, within the bound.
A program may use at most 192 MiB of HBM per device.

v0:
```python
import jax
import jax.numpy as jnp
from jax import lax
from jax.sharding import PartitionSpec as P

BF = jnp.bfloat16
F32 = jnp.float32


def dot(a, b, dims=((1,), (0,)), precision=None):
    return lax.dot_general(a, b, (dims, ((), ())), preferred_element_type=F32, precision=precision)


def swap(x, axis):
    return lax.all_to_all(x, axis, split_axis=0, concat_axis=0, tiled=True)


def per_device(
    features,
    w_self,
    basis_mats,
    basis_coeffs,
    group_rels,
    rel_local,
    edge_src,
    edge_dst,
    block_counts,
    cotangent,
):
    n_ent, width = features.shape
    ent_count = lax.axis_size("ent")
    rel_count = lax.axis_size("rel")
    slots = rel_local.shape[0]
    cap = slots // ent_count
    bases = basis_coeffs.shape[1]
    rels = basis_coeffs.shape[0]
    part = width // rel_count
    q = lax.axis_index("rel")
    s = lax.axis_index("ent")
    all_slots = slots * rel_count
    pos = jnp.arange(slots, dtype=jnp.int32)
    limits = jnp.repeat(block_counts.reshape(ent_count), cap, total_repeat_length=slots)
    live = pos % cap < limits
    src_own = edge_src - s * n_ent
    dst_own = jnp.where(live, edge_dst - pos // cap * n_ent, n_ent)
    rel_own = group_rels[rel_local]
    meta = jnp.stack([src_own, dst_own, rel_own])
    meta = lax.all_gather(meta, "rel").reshape(rel_count, 3, ent_count, cap)
    meta = meta.transpose(2, 1, 0, 3)
    src = meta[:, 0].reshape(all_slots)
    arrived = swap(meta[:, 1:], "ent")
    dst = arrived[:, 0].reshape(all_slots)
    rel = arrived[:, 1].reshape(all_slots)
    ids = jnp.arange(n_ent, dtype=jnp.int32)[:, None]
    pick_src = (ids == src[None, :]).astype(BF)
    feat_part = lax.dynamic_slice_in_dim(features, q * part, part, 1)
    rows = dot(pick_src, feat_part, ((0,), (0,))).astype(BF)
    rows = swap(rows.reshape(ent_count, rel_count * cap, part), "ent").reshape(all_slots, part)
    pick_rel = (jnp.arange(rels, dtype=jnp.int32)[:, None] == rel[None, :]).astype(F32)
    coef_t = dot(basis_coeffs, pick_rel, ((0,), (0,)), lax.Precision.HIGHEST)
    pick = (ids == dst[None, :]).astype(BF)
    degree = jnp.sum(pick, axis=1, dtype=F32)
    inverse = (1.0 / jnp.maximum(degree, 1.0))[:, None]
    mixed_t = (
        (coef_t[:, None, :] * rows.T.astype(F32)[None]).reshape(bases * part, all_slots).astype(BF)
    )
    agg = dot(pick, mixed_t, ((1,), (1,))).astype(BF)
    basis_part = lax.dynamic_slice_in_dim(
        basis_mats.reshape(bases, width, width), q * part, part, 1
    ).reshape(bases * part, width)
    partial = dot(agg, basis_part).astype(BF)
    partial = swap(partial.reshape(n_ent, rel_count, part).transpose(1, 0, 2), "rel")
    sums = jnp.sum(partial.astype(F32), axis=0)
    w_part = lax.dynamic_slice_in_dim(w_self, q * part, part, 1)
    cot = lax.dynamic_slice_in_dim(cotangent, q * part, part, 1).astype(F32)
    pre = dot(features, w_part) + sums * inverse
    sig = jax.nn.sigmoid(pre)
    act = (pre * sig).astype(BF)
    grad_pre = (cot * (sig * (1.0 + pre * (1.0 - sig)))).astype(BF)
    act = lax.all_gather(act, "rel", axis=1, tiled=True)
    grad_pre = lax.all_gather(grad_pre, "rel", axis=1, tiled=True)
    scaled = (grad_pre.astype(F32) * inverse).astype(BF)
    basis_terms = dot(agg, scaled, ((0,), (0,))).astype(BF)
    basis_terms = swap(basis_terms.reshape(ent_count, part, width), "ent")
    block = jnp.sum(basis_terms.astype(F32), axis=0)
    per_rel = bases // rel_count
    routes = [
        (r * ent_count + b, b // per_rel * ent_count + b % per_rel * rel_count + r)
        for r in range(rel_count)
        for b in range(bases)
    ]
    grad_basis = lax.ppermute(block, ("rel", "ent"), routes)
    back_t = dot(basis_part, scaled, ((1,), (1,))).astype(BF)
    spread = dot(back_t, pick).reshape(bases, part, all_slots)
    grad_rows = jnp.sum(spread * coef_t[:, None, :], axis=0).astype(BF).T
    grad_rows = swap(grad_rows.reshape(ent_count, rel_count * cap, part), "ent")
    w_rows = lax.dynamic_slice_in_dim(w_self, q * part, part, 0)
    grad_part = dot(grad_pre, w_rows, ((1,), (1,))) + dot(
        pick_src, grad_rows.reshape(all_slots, part)
    )
    grad_features = lax.all_gather(grad_part.astype(BF), "rel", axis=1, tiled=True)
    return (act, grad_features, grad_basis)


def solution(mesh):
    placed = (
        P("ent", None),
        P(),
        P(),
        P(),
        P("rel"),
        P(("rel", "ent")),
        P(("rel", "ent")),
        P(("rel", "ent")),
        P("rel", "ent", None),
        P("ent", None),
    )
    return jax.shard_map(
        per_device,
        mesh=mesh,
        in_specs=placed,
        out_specs=(P("ent", None), P("ent", None), P(("rel", "ent"), None)),
        check_vma=False,
    )
```

profile of v0, /device:TPU:27, one launch (start us, length us, event | category | flops | bytes accessed | tf_op | source)
XLA Modules:
  0.0 229.3 jit_solution(15646126451064702323)
XLA Ops:
  0.7 1.8 fusion.33
  2.5 2.1 fusion.32
  4.6 0.7 compare_select_fusion.7
  5.3 0.8 add_add_fusion.1
  6.0 4.5 %compare_select_fusion.1 = (s32[512,1]{0,1:T(1,128)S(1)}, s32[512,1]{0,1:T(1,128)S(1)}) fusion(s32[]{:T(128)} %bitcast.31, s32[]{:T(128)} %bitcast.32, s32[]{:T(128)} %bitcast.33, s32[]{:T(128)} %bitcast.34, s32[]{:T(128)} %bitcast.35, s32[]{:T(128)} %bitcast.37, s32[]{:T(128)} %bitcast.36, s32[512,1]{0,1:T(1,128)S(1)} %bitcast.106, s32[512,1]{0,1:T(1,128)S(1)} %bitcast.105), kind=kLoop, calls=%fused_computation.66 | loop fusion | flops 7168 | bytes 8220 | tf_op jit(solution)/shard_map/jit(_take)/gather | solution.py:42
  10.5 0.2 compare_reduce_fusion.24
  10.7 0.7 broadcast_subtract_fusion
  11.4 3.6 %gather_fusion = s32[512]{0:T(512)S(1)} fusion(s32[250]{0:T(256)} %param.16, s32[1024]{0:T(1024)S(1)} %pad_clamp_fusion), kind=kCustom, calls=%fused_computation | custom fusion | bytes 6144 | tf_op jit(solution)/shard_map/gather | solution.py:46
  15.0 16.4 %fusion.23 = s32[512]{0:T(512)S(1)} fusion(s32[512]{0:T(512)} %param.19, pred[512]{0:T(512)(128)(4,1)S(1)} %get-tuple-element.51, pred[512]{0:T(512)(128)(4,1)S(1)} %get-tuple-element.50, pred[512]{0:T(512)(128)(4,1)S(1)} %get-tuple-element.49, pred[512]{0:T(512)(128)(4,1)S(1)} %get-tuple-element.48, pred[512]{0:T(512)(128)(4,1)S(1)} %get-tuple-element.47, ...), kind=kLoop, calls=%fused_computation.85 | loop fusion | flops 25600 | bytes 21108 | tf_op jit(solution)/shard_map/jit(_where)/select_n | solution.py:45
  31.4 10.5 %all-gather.1 = s32[4,3,512]{2,1,0:T(4,128)S(1)} all-gather(s32[1,3,512]{2,1,0:T(4,128)S(1)} %add_bitcast_fusion), channel_id=2, replica_groups=mesh['rel'=4,'ent'=32] {'rel'}, dimensions={0}, use_global_device_ids=true | all-gather | bytes 30720 | tf_op jit(solution)/shard_map/all_gather | solution.py:48
  42.1 0.7 reshape.365
  42.9 10.3 %all-to-all-start = ((s32[32,1,128]{2,1,0:T(1,128)}), s32[32,1,128]{2,1,0:T(1,128)S(1)}, u32[]{:S(2)}, u32[]{:S(2)}) async-start(s32[32,1,128]{2,1,0:T(1,128)} %reshape.365), calls=%async_computation | async-start | bytes 32768 | tf_op jit(solution)/shard_map/all_to_all | solution.py:15
  53.3 2.1 fusion.6
  55.4 1.9 all-to-all-done
  57.3 7.0 %all-to-all-start.1 = ((bf16[32,64,128]{2,1,0:T(8,128)(2,1)}), bf16[32,64,128]{2,1,0:T(8,128)(2,1)S(1)}, u32[]{:S(2)}, u32[]{:S(2)}) async-start(bf16[32,64,128]{2,1,0:T(8,128)(2,1)} %bitcast.44), calls=%async_computation.1 | async-start | bytes 1048576 | tf_op jit(solution)/shard_map/all_to_all | solution.py:15
  64.3 4.6 %constant_dynamic-slice_fusion.1 = bf16[32,128,512]{2,1,0:T(8,128)(2,1)} fusion(bf16[32,512,512]{2,1,0:T(8,128)(2,1)} %bitcast.98, s32[]{:T(128)S(6)} %select_n.47), kind=kLoop, calls=%fused_computation.95 | loop fusion | bytes 8388612 | tf_op jit(solution)/shard_map/dynamic_slice | solution.py:68
  68.9 0.5 broadcast.362
  69.4 0.7 reduce.52
  70.1 0.1 reshape.366
  70.5 3.0 %fusion.7 = f32[32,2048]{1,0:T(8,128)S(1)} fusion(f32[1000,32]{0,1:T(8,128)S(1)} %copy-done.4, s32[2048]{0:T(1024)S(1)} %eq.52), kind=kOutput, calls=%fused_computation.18 | convolution fusion | flops 788480000 | bytes 398336 | tf_op jit(solution)/shard_map/dot_general | solution.py:11
  73.6 0.3 copy.32
  73.9 6.8 %multiply_convert_fusion = bf16[32,128,2048]{2,1,0:T(8,128)(2,1)} fusion(f32[128,2048]{1,0:T(8,128)S(1)} %bitcast.93, f32[32,2048]{1,0:T(8,128)S(1)} %fusion.7), kind=kLoop, calls=%fused_computation.2 | loop fusion | flops 16777216 | bytes 18087936 | tf_op jit(solution)/shard_map/convert_element_type | solution.py:65
  80.8 13.9 %convolution_convert_fusion = bf16[512,4096]{1,0:T(8,128)(2,1)} fusion(bf16[4096,2048]{1,0:T(8,128)(2,1)} %bitcast.92, s32[2048]{0:T(1024)S(1)} %eq.48), kind=kOutput, calls=%fused_computation.6 | convolution fusion | flops 8593080320 | bytes 20979712 | tf_op jit(solution)/shard_map/dot_general | solution.py:11
  94.7 5.5 %convolution_convert_fusion.3 = bf16[512,512]{0,1:T(8,128)(2,1)} fusion(bf16[512,4096]{1,0:T(8,128)(2,1)} %convolution_convert_fusion, bf16[4096,512]{1,0:T(8,128)(2,1)S(1)} %bitcast.95), kind=kOutput, calls=%fused_computation.23 | convolution fusion | flops 2147745792 | bytes 8912896 | tf_op jit(solution)/shard_map/dot_general | solution.py:11
  100.1 3.8 %all-to-all-start.2 = ((bf16[4,512,128]{1,2,0:T(8,128)(2,1)}), bf16[4,512,128]{1,2,0:T(8,128)(2,1)S(1)}, u32[]{:S(2)}, u32[]{:S(2)}) async-start(bf16[4,512,128]{1,2,0:T(8,128)(2,1)} %bitcast.51), calls=%async_computation.2 | async-start | bytes 1048576 | tf_op jit(solution)/shard_map/all_to_all | solution.py:15
  104.0 0.9 constant_dynamic-slice_fusion
  105.0 0.5 convert_reduce_fusion.1
  105.5 7.4 %all-to-all-done.2 = bf16[4,512,128]{1,2,0:T(8,128)(2,1)S(1)} async-done(((bf16[4,512,128]{1,2,0:T(8,128)(2,1)}), bf16[4,512,128]{1,2,0:T(8,128)(2,1)S(1)}, u32[]{:S(2)}, u32[]{:S(2)}) %all-to-all-start.2) | async-done | bytes 524320 | tf_op jit(solution)/shard_map/all_to_all | solution.py:15
  113.0 0.4 multiply_convert_fusion.6
  113.4 10.7 %all_gather.18 = bf16[512,512]{0,1:T(8,128)(2,1)S(1)} all-gather(bf16[512,128]{0,1:T(8,128)(2,1)S(1)} %get-tuple-element.54), channel_id=1, replica_groups=mesh['rel'=4,'ent'=32] {'rel'}, dimensions={1}, use_global_device_ids=true | all-gather | bytes 655360 | tf_op jit(solution)/shard_map/all_gather | solution.py:81
  124.1 6.6 %convolution_convert_fusion.1 = bf16[4096,512]{1,0:T(8,128)(2,1)} fusion(bf16[512,4096]{1,0:T(8,128)(2,1)} %convolution_convert_fusion, bf16[512,512]{0,1:T(8,128)(2,1)S(1)} %all_gather.18, f32[512]{0:T(512)S(1)} %maximum_divide_fusion), kind=kOutput, calls=%fused_computation.7 | convolution fusion | flops 2150367232 | bytes 8914944 | tf_op jit(solution)/shard_map/dot_general | solution.py:11
  130.8 11.3 %all-to-all-start.4 = ((bf16[32,128,512]{2,1,0:T(8,128)(2,1)}), bf16[32,128,512]{2,1,0:T(8,128)(2,1)}, u32[]{:S(2)}, u32[]{:S(2)}) async-start(bf16[32,128,512]{2,1,0:T(8,128)(2,1)} %bitcast.96), calls=%async_computation.4 | async-start | bytes 8388608 | tf_op jit(solution)/shard_map/all_to_all | solution.py:15
  142.1 11.1 %all_gather.17 = bf16[512,512]{0,1:T(8,128)(2,1)S(1)} all-gather(bf16[512,128]{0,1:T(8,128)(2,1)S(1)} %get-tuple-element.55), channel_id=1, replica_groups=mesh['rel'=4,'ent'=32] {'rel'}, dimensions={1}, use_global_device_ids=true | all-gather | bytes 655360 | tf_op jit(solution)/shard_map/all_gather | solution.py:80
  153.2 1.0 copy.35
  154.2 4.5 %convolution_convert_fusion.2.clone.5 = bf16[4096,512]{1,0:T(8,128)(2,1)S(1)} fusion(bf16[4096,512]{1,0:T(8,128)(2,1)} %bitcast.94, bf16[512,512]{0,1:T(8,128)(2,1)S(1)} %all_gather.18, f32[512]{0:T(512)S(1)} %maximum_divide_fusion), kind=kOutput, calls=%fused_computation.8.clone.clone.clone.2 | convolution fusion | flops 2150367232 | bytes 8914944 | tf_op jit(solution)/shard_map/dot_general | solution.py:11
  158.7 14.6 %fusion.3 = f32[4096,2048]{1,0:T(8,128)} fusion(s32[2048]{0:T(1024)S(1)} %eq.48, bf16[4096,512]{1,0:T(8,128)(2,1)S(1)} %convolution_convert_fusion.2.clone.5), kind=kOutput, calls=%fused_computation.14 | convolution fusion | flops 8590983168 | bytes 37756928 | tf_op jit(solution)/shard_map/dot_general | solution.py:11
  173.3 12.5 %multiply_reduce_fusion = bf16[128,2048]{1,0:T(8,128)(2,1)S(1)} fusion(f32[32,128,2048]{2,1,0:T(8,128)} %bitcast.91, f32[32,2048]{1,0:T(8,128)S(1)} %fusion.7), kind=kLoop, calls=%fused_computation.1 | loop fusion | flops 16515072 | bytes 34340864 | tf_op jit(solution)/shard_map/reduce_sum | solution.py:95
  185.8 1.0 copy.34
  186.8 5.1 %all-to-all-done.4 = bf16[32,128,512]{2,1,0:T(8,128)(2,1)} async-done(((bf16[32,128,512]{2,1,0:T(8,128)(2,1)}), bf16[32,128,512]{2,1,0:T(8,128)(2,1)}, u32[]{:S(2)}, u32[]{:S(2)}) %all-to-all-start.4) | async-done | bytes 4194336 | tf_op jit(solution)/shard_map/all_to_all | solution.py:15
  191.9 7.6 %all-to-all-start.3 = ((bf16[32,64,128]{2,1,0:T(8,128)(2,1)}), bf16[32,64,128]{2,1,0:T(8,128)(2,1)S(1)}, u32[]{:S(2)}, u32[]{:S(2)}) async-start(bf16[32,64,128]{2,1,0:T(8,128)(2,1)} %bitcast.54), calls=%async_computation.3 | async-start | bytes 1048576 | tf_op jit(solution)/shard_map/all_to_all | solution.py:15
  199.5 0.3 fusion.15
  199.9 2.8 %convert_reduce_fusion = f32[128,512]{1,0:T(8,128)S(1)} fusion(bf16[32,128,512]{2,1,0:T(8,128)(2,1)} %all-to-all-done.4), kind=kLoop, calls=%fused_computation.3 | loop fusion | flops 4128768 | bytes 4456448 | tf_op jit(solution)/shard_map/reduce_sum | solution.py:85
  202.7 4.7 %collective-permute-start = (f32[128,512]{1,0:T(8,128)S(1)}, f32[128,512]{1,0:T(8,128)S(1)}, u32[]{:S(2)}, u32[]{:S(2)}) collective-permute-start(f32[128,512]{1,0:T(8,128)S(1)} %convert_reduce_fusion), channel_id=1, source_target_pairs={{0,0},{1,4},{2,8},{3,12},{4,16},{5,20},{6,24},{7,28},{8,32},{9,36}... | collective-permute-start | bytes 786440 | tf_op jit(solution)/shard_map/ppermute | solution.py:92
  207.4 1.2 all-to-all-done.3
  208.6 0.9 fusion.14
  209.5 18.3 %all_gather.19 = bf16[512,512]{1,0:T(8,128)(2,1)S(1)} all-gather(bf16[512,128]{1,0:T(8,128)(2,1)S(1)} %fusion.14), channel_id=1, replica_groups=mesh['rel'=4,'ent'=32] {'rel'}, dimensions={1}, use_global_device_ids=true | all-gather | bytes 655360 | tf_op jit(solution)/shard_map/all_gather | solution.py:101
  227.8 0.8 copy.39
  228.6 0.7 copy.40
  (29 shorter events, 1.0 us)
Async XLA Ops:
  0.6 52.7 %copy-start = (bf16[512,512]{1,0:T(8,128)(2,1)S(1)}, bf16[512,512]{1,0:T(8,128)(2,1)}, u32[]{:S(2)}) copy-start(bf16[512,512]{1,0:T(8,128)(2,1)} %param.12) | copy-start | bytes 1572868
  42.9 14.5 %all-to-all-start = ((s32[32,1,128]{2,1,0:T(1,128)}), s32[32,1,128]{2,1,0:T(1,128)S(1)}, u32[]{:S(2)}, u32[]{:S(2)}) async-start(s32[32,1,128]{2,1,0:T(1,128)} %reshape.365), calls=%async_computation | async-start | bytes 32768 | tf_op jit(solution)/shard_map/all_to_all | solution.py:15
  57.3 16.1 %all-to-all-start.1 = ((bf16[32,64,128]{2,1,0:T(8,128)(2,1)}), bf16[32,64,128]{2,1,0:T(8,128)(2,1)S(1)}, u32[]{:S(2)}, u32[]{:S(2)}) async-start(bf16[32,64,128]{2,1,0:T(8,128)(2,1)} %bitcast.44), calls=%async_computation.1 | async-start | bytes 1048576 | tf_op jit(solution)/shard_map/all_to_all | solution.py:15
  64.3 6.2 %copy-start.4 = (f32[1000,32]{0,1:T(8,128)S(1)}, f32[1000,32]{0,1:T(8,128)}, u32[]{:S(2)}) copy-start(f32[1000,32]{0,1:T(8,128)} %param.15) | copy-start | bytes 384004
  80.7 13.9 %copy-start.2 = (bf16[32,128,512]{2,1,0:T(8,128)(2,1)S(1)}, bf16[32,128,512]{2,1,0:T(8,128)(2,1)}, u32[]{:S(2)}) copy-start(bf16[32,128,512]{2,1,0:T(8,128)(2,1)} %constant_dynamic-slice_fusion.1) | copy-start | bytes 12582916
  94.7 18.3 %copy-start.3 = (bf16[512,512]{1,0:T(8,128)(2,1)S(1)}, bf16[512,512]{1,0:T(8,128)(2,1)}, u32[]{:S(2)}) copy-start(bf16[512,512]{1,0:T(8,128)(2,1)} %param.13) | copy-start | bytes 1572868
  100.1 12.8 %all-to-all-start.2 = ((bf16[4,512,128]{1,2,0:T(8,128)(2,1)}), bf16[4,512,128]{1,2,0:T(8,128)(2,1)S(1)}, u32[]{:S(2)}, u32[]{:S(2)}) async-start(bf16[4,512,128]{1,2,0:T(8,128)(2,1)} %bitcast.51), calls=%async_computation.2 | async-start | bytes 1048576 | tf_op jit(solution)/shard_map/all_to_all | solution.py:15
  130.8 61.1 %all-to-all-start.4 = ((bf16[32,128,512]{2,1,0:T(8,128)(2,1)}), bf16[32,128,512]{2,1,0:T(8,128)(2,1)}, u32[]{:S(2)}, u32[]{:S(2)}) async-start(bf16[32,128,512]{2,1,0:T(8,128)(2,1)} %bitcast.96), calls=%async_computation.4 | async-start | bytes 8388608 | tf_op jit(solution)/shard_map/all_to_all | solution.py:15
  191.9 16.7 %all-to-all-start.3 = ((bf16[32,64,128]{2,1,0:T(8,128)(2,1)}), bf16[32,64,128]{2,1,0:T(8,128)(2,1)S(1)}, u32[]{:S(2)}, u32[]{:S(2)}) async-start(bf16[32,64,128]{2,1,0:T(8,128)(2,1)} %bitcast.54), calls=%async_computation.3 | async-start | bytes 1048576 | tf_op jit(solution)/shard_map/all_to_all | solution.py:15
  199.5 29.8 %copy-start.1 = (bf16[512,512]{1,0:T(8,128)(2,1)S(1)}, bf16[512,512]{1,0:T(8,128)(2,1)}, u32[]{:S(2)}) copy-start(bf16[512,512]{1,0:T(8,128)(2,1)} %param.12) | copy-start | bytes 1572868
  202.7 25.1 %collective-permute-start = (f32[128,512]{1,0:T(8,128)S(1)}, f32[128,512]{1,0:T(8,128)S(1)}, u32[]{:S(2)}, u32[]{:S(2)}) collective-permute-start(f32[128,512]{1,0:T(8,128)S(1)} %convert_reduce_fusion), channel_id=1, source_target_pairs={{0,0},{1,4},{2,8},{3,12},{4,16},{5,20},{6,24},{7,28},{8,32},{9,36}... | collective-permute-start | bytes 786440 | tf_op jit(solution)/shard_map/ppermute | solution.py:92
where the time goes:
time: 230 us; the launch traced here: 229 us
  matrix products  51.8 us (23%)
  blocking collectives  50.6 us (22%)
  other arithmetic  46.6 us (20%)
  starting transfers between devices  44.7 us (19%)
  local copies, waits for them, and re-layouts  19 us (8%)
  waiting for transfers between devices  15.7 us (7%)
    dot_general x10, matrix products, dot(): lax.dot_general(a, b, (dims, ((), ())), preferred_element_type=F32, preci...  51.8 us
    all_to_all x5, starting transfers between devices, swap(): return lax.all_to_all(x, axis, split_axis=0, concat_axis=0, tiled=True)  40 us
    all_gather x1, blocking collectives, per_device(): lax.all_gather(grad_part.astype(BF), 'rel', axis=1, tiled=True)  18.3 us
    select_n x1, other arithmetic, per_device(): dst_own = jnp.where(live, edge_dst - pos // cap * n_ent, n_ent)  16.4 us
    all_to_all x5, waiting for transfers between devices, swap(): return lax.all_to_all(x, axis, split_axis=0, concat_axis=0, tiled=True)  15.7 us
    reduce_sum x1, other arithmetic, per_device(): grad_rows = jnp.sum(spread * coef_t[:, None, :], axis=0).astype(BF).T  12.5 us
    all_gather x1, blocking collectives, per_device(): act = lax.all_gather(act, 'rel', axis=1, tiled=True)  11.1 us
    all_gather x1, blocking collectives, per_device(): grad_pre = lax.all_gather(grad_pre, 'rel', axis=1, tiled=True)  10.7 us
  transfers between devices with their start and end apart: 6, of which 4 were waited for; matrix products, arithmetic and copies ran while one was open for 22% of the time, Pallas kernels for 0%

commit v1 on v0

--- a/solution.py
+++ b/solution.py
@@ -77,8 +77,11 @@
     sig = jax.nn.sigmoid(pre)
     act = (pre * sig).astype(BF)
     grad_pre = (cot * (sig * (1.0 + pre * (1.0 - sig)))).astype(BF)
-    act = lax.all_gather(act, "rel", axis=1, tiled=True)
-    grad_pre = lax.all_gather(grad_pre, "rel", axis=1, tiled=True)
+    act, grad_pre = jnp.split(
+        lax.all_gather(jnp.concatenate([act, grad_pre], axis=0), "rel", axis=1, tiled=True),
+        [act.shape[0]],
+        axis=0,
+    )
     scaled = (grad_pre.astype(F32) * inverse).astype(BF)
     basis_terms = dot(agg, scaled, ((0,), (0,))).astype(BF)
     basis_terms = swap(basis_terms.reshape(ent_count, part, width), "ent")

time: 230 us -> 252 us (1.096)
  waiting for transfers between devices: 15.7 us -> 49.8 us
  blocking collectives: 50.6 us -> 28.7 us
  between operations: 0.92 us -> 14.3 us
  matrix products: 51.8 us -> 48.3 us
    all_gather x0 -> x1, waiting for transfers between devices: none -> 23.5 us  [per_device(): lax.all_gather(jnp.concatenate([act, grad_pre], axis=0), 'rel', axis=1, t...]
    all_gather x2 -> x0, blocking collectives: 21.8 us -> none  [the longest x1 11.1 us: per_device(): act = lax.all_gather(act, 'rel', axis=1, tiled=True)]
    all_to_all x5, waiting for transfers between devices: 15.7 us -> 26.3 us  [swap(): return lax.all_to_all(x, axis, split_axis=0, concat_axis=0, tiled=True)]
    dot_general x10, matrix products: 51.8 us -> 48.3 us  [dot(): lax.dot_general(a, b, (dims, ((), ())), preferred_element_type=F32, preci...]
  transfers between devices with their start and end apart: 6 -> 7, of which waited for: 4 -> 5; matrix products, arithmetic and copies ran while one was open for 22% -> 20% of each run, Pallas kernels for 0% -> 0%
where the time goes in v1:
time: 252 us; the launch traced here: 250 us
  waiting for transfers between devices  49.8 us (20%)
  matrix products  48.3 us (19%)
  other arithmetic  47.3 us (19%)
  starting transfers between devices  42.7 us (17%)
  blocking collectives  28.7 us (11%)
  local copies, waits for them, and re-layouts  19 us (8%)
  between operations  14.3 us (6%)
    dot_general x10, matrix products, dot(): lax.dot_general(a, b, (dims, ((), ())), preferred_element_type=F32, preci...  48.3 us
    all_to_all x5, starting transfers between devices, swap(): return lax.all_to_all(x, axis, split_axis=0, concat_axis=0, tiled=True)  37.5 us
    all_to_all x5, waiting for transfers between devices, swap(): return lax.all_to_all(x, axis, split_axis=0, concat_axis=0, tiled=True)  26.3 us
    all_gather x1, waiting for transfers between devices, per_device(): lax.all_gather(jnp.concatenate([act, grad_pre], axis=0), 'rel', axis=1, t...  23.5 us
    all_gather x1, blocking collectives, per_device(): lax.all_gather(grad_part.astype(BF), 'rel', axis=1, tiled=True)  18.2 us
    select_n x1, other arithmetic, per_device(): dst_own = jnp.where(live, edge_dst - pos // cap * n_ent, n_ent)  16.4 us
    reduce_sum x1, other arithmetic, per_device(): grad_rows = jnp.sum(spread * coef_t[:, None, :], axis=0).astype(BF).T  12.5 us
    all_gather x1, blocking collectives, per_device(): meta = lax.all_gather(meta, 'rel').reshape(rel_count, 3, ent_count, cap)  10.5 us
  transfers between devices with their start and end apart: 7, of which 5 were waited for; matrix products, arithmetic and copies ran while one was open for 20% of the time, Pallas kernels for 0%

profile of v1, /device:TPU:27, one launch (start us, length us, event | category | flops | bytes accessed | tf_op | source)
XLA Modules:
  0.0 250.2 jit_solution(15186833405366950322)
XLA Ops:
  7.2 1.8 fusion.34
  9.0 2.1 fusion.33
  11.1 0.7 compare_select_fusion.7
  11.8 0.8 add_add_fusion.1
  12.6 4.5 %compare_select_fusion.1 = (s32[512,1]{0,1:T(1,128)S(1)}, s32[512,1]{0,1:T(1,128)S(1)}) fusion(s32[]{:T(128)} %bitcast.31, s32[]{:T(128)} %bitcast.32, s32[]{:T(128)} %bitcast.33, s32[]{:T(128)} %bitcast.34, s32[]{:T(128)} %bitcast.35, s32[]{:T(128)} %bitcast.37, s32[]{:T(128)} %bitcast.36, s32[512,1]{0,1:T(1,128)S(1)} %bitcast.105, s32[512,1]{0,1:T(1,128)S(1)} %bitcast.104), kind=kLoop, calls=%fused_computation.68 | loop fusion | flops 7168 | bytes 8220 | tf_op jit(solution)/shard_map/jit(_take)/gather | solution.py:42
  17.0 0.2 compare_reduce_fusion.24
  17.2 0.7 broadcast_subtract_fusion
  17.9 3.6 %gather_fusion = s32[512]{0:T(512)S(1)} fusion(s32[250]{0:T(256)} %param.16, s32[1024]{0:T(1024)S(1)} %pad_clamp_fusion), kind=kCustom, calls=%fused_computation | custom fusion | bytes 6144 | tf_op jit(solution)/shard_map/gather | solution.py:46
  21.5 16.4 %fusion.24 = s32[512]{0:T(512)S(1)} fusion(s32[512]{0:T(512)} %param.19, pred[512]{0:T(512)(128)(4,1)S(1)} %get-tuple-element.51, pred[512]{0:T(512)(128)(4,1)S(1)} %get-tuple-element.50, pred[512]{0:T(512)(128)(4,1)S(1)} %get-tuple-element.49, pred[512]{0:T(512)(128)(4,1)S(1)} %get-tuple-element.48, pred[512]{0:T(512)(128)(4,1)S(1)} %get-tuple-element.47, ...), kind=kLoop, calls=%fused_computation.87 | loop fusion | flops 25600 | bytes 21108 | tf_op jit(solution)/shard_map/jit(_where)/select_n | solution.py:45
  37.9 10.5 %all-gather.1 = s32[4,3,512]{2,1,0:T(4,128)S(1)} all-gather(s32[1,3,512]{2,1,0:T(4,128)S(1)} %add_bitcast_fusion), channel_id=2, replica_groups=mesh['rel'=4,'ent'=32] {'rel'}, dimensions={0}, use_global_device_ids=true | all-gather | bytes 30720 | tf_op jit(solution)/shard_map/all_gather | solution.py:48
  48.6 0.7 reshape.365
  49.4 10.3 %all-to-all-start = ((s32[32,1,128]{2,1,0:T(1,128)}), s32[32,1,128]{2,1,0:T(1,128)S(1)}, u32[]{:S(2)}, u32[]{:S(2)}) async-start(s32[32,1,128]{2,1,0:T(1,128)} %reshape.365), calls=%async_computation | async-start | bytes 32768 | tf_op jit(solution)/shard_map/all_to_all | solution.py:15
  59.8 2.1 fusion.6
  61.9 1.9 all-to-all-done
  63.9 7.0 %all-to-all-start.1 = ((bf16[32,64,128]{2,1,0:T(8,128)(2,1)}), bf16[32,64,128]{2,1,0:T(8,128)(2,1)S(1)}, u32[]{:S(2)}, u32[]{:S(2)}) async-start(bf16[32,64,128]{2,1,0:T(8,128)(2,1)} %bitcast.44), calls=%async_computation.1 | async-start | bytes 1048576 | tf_op jit(solution)/shard_map/all_to_all | solution.py:15
  70.9 4.6 %constant_dynamic-slice_fusion.1 = bf16[32,128,512]{2,1,0:T(8,128)(2,1)} fusion(bf16[32,512,512]{2,1,0:T(8,128)(2,1)} %bitcast.97, s32[]{:T(128)S(6)} %select_n.47), kind=kLoop, calls=%fused_computation.97 | loop fusion | bytes 8388612 | tf_op jit(solution)/shard_map/dynamic_slice | solution.py:68
  75.5 0.5 broadcast.362
  76.0 0.7 reduce.52
  76.7 0.1 reshape.366
  77.0 2.9 %fusion.7 = f32[32,2048]{1,0:T(8,128)S(1)} fusion(f32[1000,32]{0,1:T(8,128)S(1)} %copy-done.5, s32[2048]{0:T(1024)S(1)} %eq.52), kind=kOutput, calls=%fused_computation.18 | convolution fusion | flops 788480000 | bytes 398336 | tf_op jit(solution)/shard_map/dot_general | solution.py:11
  80.1 0.3 copy.32
  80.5 6.8 %multiply_convert_fusion = bf16[32,128,2048]{2,1,0:T(8,128)(2,1)} fusion(f32[128,2048]{1,0:T(8,128)S(1)} %bitcast.92, f32[32,2048]{1,0:T(8,128)S(1)} %fusion.7), kind=kLoop, calls=%fused_computation.2 | loop fusion | flops 16777216 | bytes 18087936 | tf_op jit(solution)/shard_map/convert_element_type | solution.py:65
  87.3 12.6 %convolution_convert_fusion = bf16[512,4096]{1,0:T(8,128)(2,1)S(1)} fusion(bf16[4096,2048]{1,0:T(8,128)(2,1)} %bitcast.91, s32[2048]{0:T(1024)S(1)} %eq.48), kind=kOutput, calls=%fused_computation.6 | convolution fusion | flops 8593080320 | bytes 20979712 | tf_op jit(solution)/shard_map/dot_general | solution.py:11
  99.9 3.2 %convolution_convert_fusion.3 = bf16[512,512]{0,1:T(8,128)(2,1)} fusion(bf16[512,4096]{1,0:T(8,128)(2,1)S(1)} %convolution_convert_fusion, bf16[4096,512]{1,0:T(8,128)(2,1)S(1)} %bitcast.94), kind=kOutput, calls=%fused_computation.23 | convolution fusion | flops 2147745792 | bytes 8912896 | tf_op jit(solution)/shard_map/dot_general | solution.py:11
  103.1 3.9 %all-to-all-start.2 = ((bf16[4,512,128]{1,2,0:T(8,128)(2,1)}), bf16[4,512,128]{1,2,0:T(8,128)(2,1)S(1)}, u32[]{:S(2)}, u32[]{:S(2)}) async-start(bf16[4,512,128]{1,2,0:T(8,128)(2,1)} %bitcast.51), calls=%async_computation.2 | async-start | bytes 1048576 | tf_op jit(solution)/shard_map/all_to_all | solution.py:15
  107.0 0.9 constant_dynamic-slice_fusion
  108.0 0.5 convert_reduce_fusion.1
  108.5 7.4 %all-to-all-done.2 = bf16[4,512,128]{1,2,0:T(8,128)(2,1)S(1)} async-done(((bf16[4,512,128]{1,2,0:T(8,128)(2,1)}), bf16[4,512,128]{1,2,0:T(8,128)(2,1)S(1)}, u32[]{:S(2)}, u32[]{:S(2)}) %all-to-all-start.2) | async-done | bytes 524320 | tf_op jit(solution)/shard_map/all_to_all | solution.py:15
  116.0 0.4 multiply_convert_fusion.7
  116.4 0.7 pad_maximum_fusion
  117.1 23.5 %all-gather.4.cloned.1.call-done = bf16[1024,512]{0,1:T(8,128)(2,1)} async-done(((bf16[1024,128]{0,1:T(8,128)(2,1)}), bf16[1024,512]{0,1:T(8,128)(2,1)}) %all-gather.4.cloned.1.call-update) | async-done | bytes 1048592 | tf_op jit(solution)/shard_map/all_gather | solution.py:81
  140.7 6.8 %convolution_convert_fusion.1 = bf16[4096,512]{1,0:T(8,128)(2,1)} fusion(bf16[512,4096]{1,0:T(8,128)(2,1)} %copy-done.6, f32[512]{0:T(512)S(1)} %maximum_divide_fusion, bf16[1024,512]{0,1:T(8,128)(2,1)} %all-gather.4.cloned.1.call-done), kind=kOutput, calls=%fused_computation.7 | convolution fusion | flops 2150367232 | bytes 8914944 | tf_op jit(solution)/shard_map/dot_general | solution.py:11
  147.4 8.8 %all-to-all-start.4 = ((bf16[32,128,512]{2,1,0:T(8,128)(2,1)}), bf16[32,128,512]{2,1,0:T(8,128)(2,1)}, u32[]{:S(2)}, u32[]{:S(2)}) async-start(bf16[32,128,512]{2,1,0:T(8,128)(2,1)} %bitcast.95), calls=%async_computation.4 | async-start | bytes 8388608 | tf_op jit(solution)/shard_map/all_to_all | solution.py:15
  156.3 1.0 copy.35
  157.3 4.5 %convolution_convert_fusion.2.clone.5 = bf16[4096,512]{1,0:T(8,128)(2,1)S(1)} fusion(bf16[4096,512]{1,0:T(8,128)(2,1)} %bitcast.93, f32[512]{0:T(512)S(1)} %maximum_divide_fusion, bf16[1024,512]{0,1:T(8,128)(2,1)S(1)} %copy-done.3), kind=kOutput, calls=%fused_computation.8.clone.clone.clone.2 | convolution fusion | flops 2150367232 | bytes 8914944 | tf_op jit(solution)/shard_map/dot_general | solution.py:11
  161.8 14.6 %fusion.3 = f32[4096,2048]{1,0:T(8,128)} fusion(s32[2048]{0:T(1024)S(1)} %eq.48, bf16[4096,512]{1,0:T(8,128)(2,1)S(1)} %convolution_convert_fusion.2.clone.5), kind=kOutput, calls=%fused_computation.14 | convolution fusion | flops 8590983168 | bytes 37756928 | tf_op jit(solution)/shard_map/dot_general | solution.py:11
  176.4 12.5 %multiply_reduce_fusion = bf16[128,2048]{1,0:T(8,128)(2,1)S(1)} fusion(f32[32,128,2048]{2,1,0:T(8,128)} %bitcast.90, f32[32,2048]{1,0:T(8,128)S(1)} %fusion.7), kind=kLoop, calls=%fused_computation.1 | loop fusion | flops 16515072 | bytes 34340864 | tf_op jit(solution)/shard_map/reduce_sum | solution.py:98
  188.9 1.0 copy.34
  189.9 16.2 %all-to-all-done.4 = bf16[32,128,512]{2,1,0:T(8,128)(2,1)} async-done(((bf16[32,128,512]{2,1,0:T(8,128)(2,1)}), bf16[32,128,512]{2,1,0:T(8,128)(2,1)}, u32[]{:S(2)}, u32[]{:S(2)}) %all-to-all-start.4) | async-done | bytes 4194336 | tf_op jit(solution)/shard_map/all_to_all | solution.py:15
  206.1 7.6 %all-to-all-start.3 = ((bf16[32,64,128]{2,1,0:T(8,128)(2,1)}), bf16[32,64,128]{2,1,0:T(8,128)(2,1)S(1)}, u32[]{:S(2)}, u32[]{:S(2)}) async-start(bf16[32,64,128]{2,1,0:T(8,128)(2,1)} %bitcast.54), calls=%async_computation.3 | async-start | bytes 1048576 | tf_op jit(solution)/shard_map/all_to_all | solution.py:15
  213.7 0.3 fusion.15
  214.0 2.8 %convert_reduce_fusion = f32[128,512]{1,0:T(8,128)S(1)} fusion(bf16[32,128,512]{2,1,0:T(8,128)(2,1)} %all-to-all-done.4), kind=kLoop, calls=%fused_computation.3 | loop fusion | flops 4128768 | bytes 4456448 | tf_op jit(solution)/shard_map/reduce_sum | solution.py:88
  216.8 5.2 %collective-permute-start = (f32[128,512]{1,0:T(8,128)S(1)}, f32[128,512]{1,0:T(8,128)S(1)}, u32[]{:S(2)}, u32[]{:S(2)}) collective-permute-start(f32[128,512]{1,0:T(8,128)S(1)} %convert_reduce_fusion), channel_id=1, source_target_pairs={{0,0},{1,4},{2,8},{3,12},{4,16},{5,20},{6,24},{7,28},{8,32},{9,36}... | collective-permute-start | bytes 786440 | tf_op jit(solution)/shard_map/ppermute | solution.py:95
  222.0 0.7 all-to-all-done.3
  222.8 0.9 fusion.14
  223.7 18.2 %all_gather.15 = bf16[512,512]{1,0:T(8,128)(2,1)S(1)} all-gather(bf16[512,128]{1,0:T(8,128)(2,1)S(1)} %fusion.14), channel_id=1, replica_groups=mesh['rel'=4,'ent'=32] {'rel'}, dimensions={1}, use_global_device_ids=true | all-gather | bytes 655360 | tf_op jit(solution)/shard_map/all_gather | solution.py:104
  241.9 0.8 copy.39
  242.7 0.7 copy.40
  (37 shorter events, 1.0 us)
Async XLA Ops:
  7.2 52.7 %copy-start = (bf16[512,512]{1,0:T(8,128)(2,1)S(1)}, bf16[512,512]{1,0:T(8,128)(2,1)}, u32[]{:S(2)}) copy-start(bf16[512,512]{1,0:T(8,128)(2,1)} %param.12) | copy-start | bytes 1572868
  49.4 14.5 %all-to-all-start = ((s32[32,1,128]{2,1,0:T(1,128)}), s32[32,1,128]{2,1,0:T(1,128)S(1)}, u32[]{:S(2)}, u32[]{:S(2)}) async-start(s32[32,1,128]{2,1,0:T(1,128)} %reshape.365), calls=%async_computation | async-start | bytes 32768 | tf_op jit(solution)/shard_map/all_to_all | solution.py:15
  63.9 16.1 %all-to-all-start.1 = ((bf16[32,64,128]{2,1,0:T(8,128)(2,1)}), bf16[32,64,128]{2,1,0:T(8,128)(2,1)S(1)}, u32[]{:S(2)}, u32[]{:S(2)}) async-start(bf16[32,64,128]{2,1,0:T(8,128)(2,1)} %bitcast.44), calls=%async_computation.1 | async-start | bytes 1048576 | tf_op jit(solution)/shard_map/all_to_all | solution.py:15
  70.8 6.2 %copy-start.5 = (f32[1000,32]{0,1:T(8,128)S(1)}, f32[1000,32]{0,1:T(8,128)}, u32[]{:S(2)}) copy-start(f32[1000,32]{0,1:T(8,128)} %param.15) | copy-start | bytes 384004
  87.3 12.6 %copy-start.2 = (bf16[32,128,512]{2,1,0:T(8,128)(2,1)S(1)}, bf16[32,128,512]{2,1,0:T(8,128)(2,1)}, u32[]{:S(2)}) copy-start(bf16[32,128,512]{2,1,0:T(8,128)(2,1)} %constant_dynamic-slice_fusion.1) | copy-start | bytes 12582916
  99.9 3.2 %copy-start.6 = (bf16[512,4096]{1,0:T(8,128)(2,1)}, bf16[512,4096]{1,0:T(8,128)(2,1)S(1)}, u32[]{:S(2)}) copy-start(bf16[512,4096]{1,0:T(8,128)(2,1)S(1)} %convolution_convert_fusion) | copy-start | bytes 12582916
  99.9 16.0 %copy-start.4 = (bf16[512,512]{1,0:T(8,128)(2,1)S(1)}, bf16[512,512]{1,0:T(8,128)(2,1)}, u32[]{:S(2)}) copy-start(bf16[512,512]{1,0:T(8,128)(2,1)} %param.13) | copy-start | bytes 1572868
  103.1 12.8 %all-to-all-start.2 = ((bf16[4,512,128]{1,2,0:T(8,128)(2,1)}), bf16[4,512,128]{1,2,0:T(8,128)(2,1)S(1)}, u32[]{:S(2)}, u32[]{:S(2)}) async-start(bf16[4,512,128]{1,2,0:T(8,128)(2,1)} %bitcast.51), calls=%async_computation.2 | async-start | bytes 1048576 | tf_op jit(solution)/shard_map/all_to_all | solution.py:15
  106.9 33.7 %all-gather.4.cloned.1.call-start = ((), (), s32[]{:S(2)}) async-start(), calls=%async_computation.5 | async-start | bytes 1310720 | tf_op jit(solution)/shard_map/all_gather | solution.py:81
  147.4 8.8 %slice-start = ((bf16[1024,512]{0,1:T(8,128)(2,1)}), bf16[512,512]{0,1:T(8,128)(2,1)S(1)}, s32[]{:S(2)}) async-start(bf16[1024,512]{0,1:T(8,128)(2,1)} %all-gather.4.cloned.1.call-done), calls=%async_computation.6 | async-start | bytes 1048576 | tf_op jit(solution)/shard_map/split | solution.py:80
  147.4 9.8 %copy-start.3 = (bf16[1024,512]{0,1:T(8,128)(2,1)S(1)}, bf16[1024,512]{0,1:T(8,128)(2,1)}, u32[]{:S(2)}) copy-start(bf16[1024,512]{0,1:T(8,128)(2,1)} %all-gather.4.cloned.1.call-done) | copy-start | bytes 3145732
  147.4 58.7 %all-to-all-start.4 = ((bf16[32,128,512]{2,1,0:T(8,128)(2,1)}), bf16[32,128,512]{2,1,0:T(8,128)(2,1)}, u32[]{:S(2)}, u32[]{:S(2)}) async-start(bf16[32,128,512]{2,1,0:T(8,128)(2,1)} %bitcast.95), calls=%async_computation.4 | async-start | bytes 8388608 | tf_op jit(solution)/shard_map/all_to_all | solution.py:15
  206.1 16.7 %all-to-all-start.3 = ((bf16[32,64,128]{2,1,0:T(8,128)(2,1)}), bf16[32,64,128]{2,1,0:T(8,128)(2,1)S(1)}, u32[]{:S(2)}, u32[]{:S(2)}) async-start(bf16[32,64,128]{2,1,0:T(8,128)(2,1)} %bitcast.54), calls=%async_computation.3 | async-start | bytes 1048576 | tf_op jit(solution)/shard_map/all_to_all | solution.py:15
  213.7 29.7 %copy-start.1 = (bf16[512,512]{1,0:T(8,128)(2,1)S(1)}, bf16[512,512]{1,0:T(8,128)(2,1)}, u32[]{:S(2)}) copy-start(bf16[512,512]{1,0:T(8,128)(2,1)} %param.12) | copy-start | bytes 1572868
  216.8 25.0 %collective-permute-start = (f32[128,512]{1,0:T(8,128)S(1)}, f32[128,512]{1,0:T(8,128)S(1)}, u32[]{:S(2)}, u32[]{:S(2)}) collective-permute-start(f32[128,512]{1,0:T(8,128)S(1)} %convert_reduce_fusion), channel_id=1, source_target_pairs={{0,0},{1,4},{2,8},{3,12},{4,16},{5,20},{6,24},{7,28},{8,32},{9,36}... | collective-permute-start | bytes 786440 | tf_op jit(solution)/shard_map/ppermute | solution.py:95
Sparse Core Ops, SparseCore 0:
  117.3 23.3 all-gather.3
